TPU v7x, 256 devices: a whole 4x4x8 slice. The times are simulated.
256 devices in a mesh: pair: 4 (over y_hi, core), cd: 64 (over z, x, y_lo).
Axes of the slice: x: 4, y: 4 (y_hi: 2, y_lo: 2; y = y_hi * 2 + y_lo), z: 8, core: 2. Of those that a mesh axis runs over, the one named last changes fastest.
Arguments:
- lambda_amps: bfloat16 [11264, 1024], P('pair'), may hold values from -0.0546875 to 0.0546875
- t_amps: bfloat16 [11264, 1024], P('pair', 'cd'), may hold values from -6 to 6
- coef_mu: float32 [768, 64], P('pair'), may hold values from -0.75 to 0.75
- coef_nu: float32 [768, 16], replicated, may hold values from -1.5 to 1.5
Outputs:
- half_ao: bfloat16 [768, 768, 1024], P('pair', 'cd')
All inputs are finite; a program needn't handle non-finite values.
Results may differ from a plain program's by a relative error of at most 0.001.
Values sent between devices are 32-bit elements; how exact they have to be, the bound alone decides.
A program may use at most 64 MiB of HBM per device.

v0:
```python
import jax
import jax.numpy as jnp
from jax import lax
from jax.sharding import PartitionSpec as P

A = 64
B = 16


def cut_along(array, dim, peers):
    before, after = (array.shape[:dim], array.shape[dim + 1 :])
    return jnp.moveaxis(array.reshape(*before, peers, -1, *after), dim, 0)


def sent_and_summed(array, axis, dim):
    blocks = cut_along(array, dim, lax.axis_size(axis))
    arrived = lax.all_to_all(blocks, axis, split_axis=0, concat_axis=0, tiled=True)
    return arrived.sum(axis=0)


def body(lambda_amps, t_amps, coef_mu, coef_nu):
    partial_value = lax.dot_general(
        lambda_amps, t_amps, (((0,), (0,)), ((), ())), preferred_element_type=jnp.float32
    )
    local_cols = partial_value.shape[1]
    groups = lax.axis_size("pair")
    share = sent_and_summed(partial_value.reshape(A, B * local_cols), "pair", 0)
    panel = share.reshape(A // groups, B, local_cols)
    half = jnp.einsum("abc,nb->nac", panel, coef_nu, precision=lax.Precision.HIGHEST)
    moved = lax.all_to_all(half, "cd", split_axis=0, concat_axis=2, tiled=True)
    gathered = lax.all_gather(moved, "pair", axis=1, tiled=True)
    result = jnp.einsum("ma,nac->mnc", coef_mu, gathered, precision=lax.Precision.HIGHEST)
    return result.astype(jnp.bfloat16)


def solution(mesh):
    in_specs = (P("pair", None), P("pair", "cd"), P("pair", None), P())
    out_specs = P("pair", "cd", None)
    return jax.shard_map(body, mesh=mesh, in_specs=in_specs, out_specs=out_specs, check_vma=False)
```

profile of v0, /device:TPU:1, one launch (start us, length us, event | category | flops | bytes accessed | tf_op | source)
XLA Modules:
  0.0 139.2 jit_solution(14465179184034495695)
XLA Ops:
  6.5 0.0 copy-start
  6.5 0.0 copy-start.2
  6.5 0.0 all-gather.2.cloned.1.call-start
  6.5 0.9 copy-done
  7.4 4.3 %fusion.2 = f32[1024,16]{1,0:T(8,128)S(1)} fusion(bf16[2816,1024]{1,0:T(8,128)(2,1)} %param.4, bf16[2816,16]{0,1:T(8,128)(2,1)S(1)} %copy-done), kind=kOutput, calls=%fused_computation.4 | convolution fusion | flops 92274688 | bytes 5922816 | tf_op jit(solution)/shard_map/dot_general | solution.py:22
  11.8 0.2 reshape_reshape.3
  12.0 10.5 %all_to_all.23 = f32[4,16,256]{2,1,0:T(8,128)S(1)} all-to-all(f32[4,16,256]{2,1,0:T(8,128)S(1)} %reshape_reshape.3), channel_id=1, replica_groups=mesh['pair'=4,'cd'=64] {'pair'}, dimensions={0} | all-to-all | bytes 131072 | tf_op jit(solution)/shard_map/all_to_all | solution.py:17
  22.5 0.1 reshape.3
  22.6 0.0 copy-done.2
  22.6 0.8 convolution_bitcast_fusion
  23.5 5.0 %copy.11 = f32[768,16,16]{2,1,0:T(8,128)} copy(f32[768,16,16]{0,2,1:T(8,128)S(1)} %convolution_bitcast_fusion) | data formatting | bytes 1572864 | tf_op jit(solution)/shard_map/abc,nb->nac/dot_general | solution.py:29
  28.5 4.8 %reshape.6 = f32[64,1,3072]{2,1,0:T(1,128)S(1)} reshape(f32[768,16,16]{2,1,0:T(8,128)} %copy.11) | data formatting | bytes 1572864
  33.2 32.1 %all_to_all.24 = f32[64,1,3072]{2,1,0:T(1,128)S(1)} all-to-all(f32[64,1,3072]{2,1,0:T(1,128)S(1)} %reshape.6), channel_id=1, replica_groups=mesh['pair'=4,'cd'=64] {'cd'}, dimensions={0} | all-to-all | bytes 1572864 | tf_op jit(solution)/shard_map/all_to_all | solution.py:30
  65.3 0.5 broadcast
  65.8 2.6 %reduce = f32[64,3072]{1,0:T(8,128)S(1)} reduce(f32[64,1,3072]{2,1,0:T(1,128)S(1)} %all_to_all.24, f32[]{:T(128)} %broadcast), dimensions={1}, to_apply=%all_to_all.17.reduce_sub_computation | reduce | bytes 1572868 | tf_op jit(solution)/shard_map/all_to_all | solution.py:30
  68.5 3.8 %reshape.7 = f32[768,16,16]{2,1,0:T(8,128)} reshape(f32[64,3072]{1,0:T(8,128)S(1)} %reduce) | data formatting | bytes 1572864
  72.3 9.1 %copy.13 = f32[12,16,64,16]{3,2,1,0:T(8,128)} copy(f32[12,16,64,16]{3,1,0,2:T(8,128)} %bitcast.20) | data formatting | bytes 1572864 | tf_op jit(solution)/shard_map/all_to_all | solution.py:30
  81.4 0.0 copy-start.1
  81.4 7.1 %all_to_all.20 = f32[12,16,1024]{2,1,0:T(8,128)} reshape(f32[12,16,64,16]{3,2,1,0:T(8,128)} %copy.13) | data formatting | bytes 1572864 | tf_op jit(solution)/shard_map/all_to_all | solution.py:30
  88.5 0.0 all-gather.2.cloned.1.call-update
  88.5 33.2 %all-gather.2.cloned.1.call-done = f32[12,64,1024]{2,1,0:T(8,128)} async-done(((f32[12,16,1024]{2,1,0:T(8,128)}), f32[12,64,1024]{2,1,0:T(8,128)}) %all-gather.2.cloned.1.call-update) | async-done | bytes 3145744 | tf_op jit(solution)/shard_map/all_gather | solution.py:31
  121.7 0.0 copy-done.1
  121.7 10.6 %convert_bitcast_fusion = bf16[192,12,1024]{2,0,1:T(8,128)(2,1)} fusion(f32[12,64,1024]{2,1,0:T(8,128)} %all-gather.2.cloned.1.call-done, f32[192,64]{0,1:T(8,128)S(1)} %copy-done.1), kind=kOutput, calls=%fused_computation | convolution fusion | flops 1814298624 | bytes 7913472 | tf_op jit(solution)/shard_map/ma,nac->mnc/dot_general | solution.py:32
  (1 shorter events, 0.0 us)
Async XLA Ops:
  6.5 0.9 copy-start
  6.5 16.1 %copy-start.2 = (f32[768,16]{0,1:T(8,128)S(1)}, f32[768,16]{0,1:T(8,128)}, u32[]{:S(2)}) copy-start(f32[768,16]{0,1:T(8,128)} %param.7) | copy-start | bytes 147460
  6.5 115.2 %all-gather.2.cloned.1.call-start = ((), (), s32[]{:S(2)}) async-start(), calls=%async_computation.2 | async-start | bytes 3932160 | tf_op jit(solution)/shard_map/all_gather | solution.py:31
  81.4 40.3 %copy-start.1 = (f32[192,64]{0,1:T(8,128)S(1)}, f32[192,64]{0,1:T(8,128)}, u32[]{:S(2)}) copy-start(f32[192,64]{0,1:T(8,128)} %param.6) | copy-start | bytes 147460
Sparse Core Ops, SparseCore 0:
  88.7 33.0 all-gather.1
where the time goes:
time: 140 us; the launch traced here: 139 us
  blocking collectives  42.6 us (30%)
  waiting for transfers between devices  33.2 us (24%)
  local copies, waits for them, and re-layouts  31.5 us (22%)
  matrix products  15.8 us (11%)
  between operations  13.4 us (10%)
  other arithmetic  2.61 us (2%)
    all_gather x1, waiting for transfers between devices, body(): gathered = lax.all_gather(moved, 'pair', axis=1, tiled=True)  33.2 us
    all_to_all x1, blocking collectives, body(): moved = lax.all_to_all(half, 'cd', split_axis=0, concat_axis=2, tiled=True)  32.1 us
    all_to_all x3, local copies, waits for them, and re-layouts, body(): moved = lax.all_to_all(half, 'cd', split_axis=0, concat_axis=2, tiled=True)  16.7 us
    dot_general x1, matrix products, body(): jnp.einsum('ma,nac->mnc', coef_mu, gathered, precision=lax.Precision.HIGH...  10.6 us
    all_to_all x1, blocking collectives, sent_and_summed(): lax.all_to_all(blocks, axis, split_axis=0, concat_axis=0, tiled=True)  10.5 us
    unnamed x8, local copies, waits for them, and re-layouts  9.51 us
    dot_general x1, local copies, waits for them, and re-layouts, body(): jnp.einsum('abc,nb->nac', panel, coef_nu, precision=lax.Precision.HIGHEST)  4.98 us
    dot_general x1, matrix products, body(): lax.dot_general(lambda_amps, t_amps, (((0,), (0,)), ((), ())), preferred_...  4.33 us
  transfers between devices with their start and end apart: 1, of which 1 were waited for; matrix products, arithmetic and copies ran while one was open for 0% of the time, Pallas kernels for 0%

commit v1 on v0

--- a/solution.py
+++ b/solution.py
@@ -28,7 +28,9 @@
     panel = share.reshape(A // groups, B, local_cols)
     half = jnp.einsum("abc,nb->nac", panel, coef_nu, precision=lax.Precision.HIGHEST)
     moved = lax.all_to_all(half, "cd", split_axis=0, concat_axis=2, tiled=True)
-    gathered = lax.all_gather(moved, "pair", axis=1, tiled=True)
+    gathered = jnp.concatenate(
+        lax.all_to_all(jnp.stack([moved] * lax.axis_size("pair")), "pair", 0, 0), axis=1
+    )
     result = jnp.einsum("ma,nac->mnc", coef_mu, gathered, precision=lax.Precision.HIGHEST)
     return result.astype(jnp.bfloat16)
 

time: 140 us -> 135 us (0.964)
  blocking collectives: 42.6 us -> 86.2 us
  waiting for transfers between devices: 33.2 us -> 0 us
  between operations: 13.4 us -> 0.08 us
    all_to_all x0 -> x1, blocking collectives: none -> 43.6 us  [body(): lax.all_to_all(jnp.stack([moved] * lax.axis_size('pair')), 'pair', 0, 0)]
    all_gather x1 -> x0, waiting for transfers between devices: 33.2 us -> none  [body(): gathered = lax.all_gather(moved, 'pair', axis=1, tiled=True)]
    all_to_all x3 -> x2, local copies, waits for them, and re-layouts: 16.7 us -> 9.59 us  [body(): moved = lax.all_to_all(half, 'cd', split_axis=0, concat_axis=2, tiled=True)]
    another operation x0 -> x2, local copies, waits for them, and re-layouts: none -> 6.66 us  [body(): jnp.stack([moved] * lax.axis_size('pair'))]
  transfers between devices with their start and end apart: 1 -> 0, of which waited for: 1 -> 0; matrix products, arithmetic and copies ran while one was open for 0% -> 0% of each run, Pallas kernels for 0% -> 0%
where the time goes in v1:
time: 135 us
  blocking collectives  86.2 us (64%)
  local copies, waits for them, and re-layouts  31.5 us (23%)
  matrix products  14.5 us (11%)
  other arithmetic  2.61 us (2%)
    all_to_all x1, blocking collectives, body(): lax.all_to_all(jnp.stack([moved] * lax.axis_size('pair')), 'pair', 0, 0)  43.6 us
    all_to_all x1, blocking collectives, body(): moved = lax.all_to_all(half, 'cd', split_axis=0, concat_axis=2, tiled=True)  32.1 us
    all_to_all x1, blocking collectives, sent_and_summed(): lax.all_to_all(blocks, axis, split_axis=0, concat_axis=0, tiled=True)  10.5 us
    all_to_all x2, local copies, waits for them, and re-layouts, body(): moved = lax.all_to_all(half, 'cd', split_axis=0, concat_axis=2, tiled=True)  9.59 us
    unnamed x8, local copies, waits for them, and re-layouts  9.52 us
    dot_general x1, matrix products, body(): jnp.einsum('ma,nac->mnc', coef_mu, gathered, precision=lax.Precision.HIGH...  9.32 us
    another operation x2, local copies, waits for them, and re-layouts, body(): jnp.stack([moved] * lax.axis_size('pair'))  6.66 us
    dot_general x1, local copies, waits for them, and re-layouts, body(): jnp.einsum('abc,nb->nac', panel, coef_nu, precision=lax.Precision.HIGHEST)  4.99 us

profile of v1, /device:TPU:1, one launch (start us, length us, event | category | flops | bytes accessed | tf_op | source)
XLA Modules:
  0.0 134.9 jit_solution(1001069900202482397)
XLA Ops:
  0.0 0.0 copy-start
  0.0 0.0 copy-start.2
  0.0 0.9 copy-done
  0.9 4.3 %fusion.2 = f32[1024,16]{1,0:T(8,128)S(1)} fusion(bf16[2816,1024]{1,0:T(8,128)(2,1)} %param.4, bf16[2816,16]{0,1:T(8,128)(2,1)S(1)} %copy-done), kind=kOutput, calls=%fused_computation.4 | convolution fusion | flops 92274688 | bytes 5922816 | tf_op jit(solution)/shard_map/dot_general | solution.py:22
  5.2 0.2 reshape_reshape.3
  5.5 10.5 %all_to_all.25 = f32[4,16,256]{2,1,0:T(8,128)S(1)} all-to-all(f32[4,16,256]{2,1,0:T(8,128)S(1)} %reshape_reshape.3), channel_id=1, replica_groups=mesh['pair'=4,'cd'=64] {'pair'}, dimensions={0} | all-to-all | bytes 131072 | tf_op jit(solution)/shard_map/all_to_all | solution.py:17
  16.0 0.1 reshape.12
  16.1 0.0 copy-done.2
  16.1 0.8 convolution_bitcast_fusion
  16.9 5.0 %copy.10 = f32[768,16,16]{2,1,0:T(8,128)} copy(f32[768,16,16]{0,2,1:T(8,128)S(1)} %convolution_bitcast_fusion) | data formatting | bytes 1572864 | tf_op jit(solution)/shard_map/abc,nb->nac/dot_general | solution.py:29
  21.9 4.8 %reshape.17 = f32[64,1,3072]{2,1,0:T(1,128)S(1)} reshape(f32[768,16,16]{2,1,0:T(8,128)} %copy.10) | data formatting | bytes 1572864
  26.7 32.1 %all_to_all.26 = f32[64,1,3072]{2,1,0:T(1,128)S(1)} all-to-all(f32[64,1,3072]{2,1,0:T(1,128)S(1)} %reshape.17), channel_id=1, replica_groups=mesh['pair'=4,'cd'=64] {'cd'}, dimensions={0} | all-to-all | bytes 1572864 | tf_op jit(solution)/shard_map/all_to_all | solution.py:30
  58.8 0.5 broadcast.1
  59.3 2.6 %reduce = f32[64,3072]{1,0:T(8,128)S(1)} reduce(f32[64,1,3072]{2,1,0:T(1,128)S(1)} %all_to_all.26, f32[]{:T(128)} %broadcast.1), dimensions={1}, to_apply=%all_to_all.18.reduce_sub_computation | reduce | bytes 1572868 | tf_op jit(solution)/shard_map/all_to_all | solution.py:30
  61.9 3.8 %reshape.18 = f32[768,16,16]{2,1,0:T(8,128)} reshape(f32[64,3072]{1,0:T(8,128)S(1)} %reduce) | data formatting | bytes 1572864
  65.8 9.1 %copy.12 = f32[12,16,64,16]{3,2,1,0:T(8,128)} copy(f32[12,16,64,16]{3,1,0,2:T(8,128)} %bitcast.22) | data formatting | bytes 1572864 | tf_op jit(solution)/shard_map/all_to_all | solution.py:30
  74.9 6.3 %stack.4 = f32[12,16,1024]{2,1,0:T(8,128)S(1)} reshape(f32[12,16,64,16]{3,2,1,0:T(8,128)} %copy.12) | data formatting | bytes 1572864 | tf_op jit(solution)/shard_map/stack | solution.py:32
  81.1 0.4 stack.10
  81.5 0.0 copy-start.1
  81.5 43.6 %all_to_all.27 = f32[4,12,16,1024]{3,2,1,0:T(8,128)S(1)} all-to-all(f32[4,12,16,1024]{3,2,1,0:T(8,128)S(1)} %stack.10), channel_id=1, replica_groups=mesh['pair'=4,'cd'=64] {'pair'}, dimensions={0} | all-to-all | bytes 6291456 | tf_op jit(solution)/shard_map/all_to_all | solution.py:32
  125.2 0.4 copy.13
  125.5 0.0 copy-done.1
  125.5 9.3 %convert_bitcast_fusion = bf16[192,12,1024]{2,0,1:T(8,128)(2,1)} fusion(f32[12,64,1024]{2,1,0:T(8,128)S(1)} %bitcast.24, f32[192,64]{0,1:T(8,128)S(1)} %copy-done.1), kind=kOutput, calls=%fused_computation | convolution fusion | flops 1814298624 | bytes 7913472 | tf_op jit(solution)/shard_map/ma,nac->mnc/dot_general | solution.py:34
  (1 shorter events, 0.0 us)
Async XLA Ops:
  0.0 0.9 copy-start
  0.0 16.1 %copy-start.2 = (f32[768,16]{0,1:T(8,128)S(1)}, f32[768,16]{0,1:T(8,128)}, u32[]{:S(2)}) copy-start(f32[768,16]{0,1:T(8,128)} %param.7) | copy-start | bytes 147460
  81.5 44.0 %copy-start.1 = (f32[192,64]{0,1:T(8,128)S(1)}, f32[192,64]{0,1:T(8,128)}, u32[]{:S(2)}) copy-start(f32[192,64]{0,1:T(8,128)} %param.6) | copy-start | bytes 147460
